TPU v7x, 256 devices: a whole 4x4x8 slice. The times are simulated.
256 devices in a mesh: seq: 32 (over x, y, core), head: 8 (over z).
Axes of the slice: x: 4, y: 4, z: 8, core: 2. Of those that a mesh axis runs over, the one named last changes fastest.
Arguments:
- new_states: bfloat16 [96, 1024], replicated, may hold values from -6 to 6
- lengths: int32 [24], replicated, may hold values from 1 to 16380, as said below
- cache_keys: bfloat16 [24, 16384, 1024], P(None, 'seq', 'head'), may hold values from -3000 to 3000
- cache_values: bfloat16 [24, 16384, 1024], P(None, 'seq', 'head'), may hold values from -6 to 6
- buckets: int32 [24, 4, 16384], P(None, None, 'seq'), may hold values from 0 to 31, as said below
- attn_gain: float32 [1024], replicated, may hold values from 0.25 to 1.75
- w_query: bfloat16 [1024, 1024], P(None, 'head'), may hold values from -0.0234375 to 0.0234375
- w_key: bfloat16 [1024, 1024], P(None, 'head'), may hold values from -0.1875 to 0.1875
- w_value: bfloat16 [1024, 1024], P(None, 'head'), may hold values from -0.1875 to 0.1875
- rel_bias: float32 [32, 16], P(None, 'head'), may hold values from -27 to 2
- w_out: bfloat16 [1024, 1024], P('head'), may hold values from -0.1875 to 0.1875
- ffn_gain: float32 [1024], replicated, may hold values from 0.25 to 1.75
- w_router: float32 [1024, 16], replicated, may hold values from -0.1875 to 0.1875
- w_gate: bfloat16 [16, 1024, 2816], P('head', None, 'seq'), may hold values from -0.1875 to 0.1875
- w_up: bfloat16 [16, 1024, 2816], P('head', None, 'seq'), may hold values from -0.1875 to 0.1875
- w_down: bfloat16 [16, 2816, 1024], P('head', 'seq'), may hold values from -0.109375 to 0.109375
- expert_picks: int32 [4, 24, 2], replicated, may hold values from 0 to 15, all different within a row; in each aligned block of 24 rows (0 to 23, 24 to 47, ..., all dimensions but the last counted through in order) at most 4 rows name the same one
- final_gain: float32 [1024], replicated, may hold values from 0.25 to 1.75
- w_vocab: bfloat16 [1024, 32128], P(None, 'seq'), may hold values from -0.5 to 0.5
Outputs:
- final_hidden: bfloat16 [96, 1024], P('head')
- hidden_norm: float32 [96], P('head')
- logit_max: float32 [96], P('head')
Inputs may be any that keep to these rules, and one draw needn't show every extreme that they name: `lengths`: some request has exactly 16380 cached positions. buckets[r, t, p] is the T5 relative position bucket (16 exact buckets, then logarithmic up to a distance of 128) of the distance lengths[r] + t - p where that is not negative, else 0. `expert_picks`: A request's two picks at a step differ; at each step no expert is picked by more than 4 requests, a bound that some block reaches.
All inputs are finite; a program needn't handle non-finite values.
Results may differ from a plain program's by a relative error of at most 0.0096.
Values may be sent and summed in bfloat16 or wider, within the bound.
A program may use at most 64 MiB of HBM per device.

v0:
```python
import jax
import jax.numpy as jnp
from jax import lax
from jax.sharding import PartitionSpec as P

CAP = 4


def joined(part, axis, combine):
    gathered = jax.tree.map(lambda a: lax.all_gather(a, axis), part)

    def take(source):
        return jax.tree.map(lambda a: lax.dynamic_index_in_dim(a, source, 0, False), gathered)

    return lax.fori_loop(
        1, lax.axis_size(axis), lambda source, state: combine(state, take(source)), take(0)
    )


def norm_parts(values, gain_row):
    norm_root = jnp.sqrt(jnp.mean(values * values, axis=-1, keepdims=True) + 1e-06)
    return (values / norm_root * gain_row, norm_root[..., 0])


def join_three(earlier_part, later_part):
    joint_top = jnp.maximum(earlier_part[0], later_part[0])
    lead_scale = jnp.exp(earlier_part[0] - joint_top)
    trail_scale = jnp.exp(later_part[0] - joint_top)
    mass = earlier_part[1] * lead_scale + later_part[1] * trail_scale
    weighted = earlier_part[2] * lead_scale[..., None] + later_part[2] * trail_scale[..., None]
    return (joint_top, mass, weighted)


def shards(
    new_states,
    lengths,
    cache_keys,
    cache_values,
    buckets,
    attn_gain,
    w_query,
    w_key,
    w_value,
    rel_bias,
    w_out,
    ffn_gain,
    w_router,
    w_gate,
    w_up,
    w_down,
    expert_picks,
    final_gain,
    w_vocab,
):
    seq_count = lax.axis_size("seq")
    head_count = lax.axis_size("head")
    seq_index = lax.axis_index("seq")
    head_index = lax.axis_index("head")
    requests, span_local, inner_local = cache_keys.shape
    tokens = new_states.shape[0]
    step_count = tokens // requests
    bucket_count, heads_local = rel_bias.shape
    head_dim = inner_local // heads_local
    states = new_states.astype(jnp.float32)
    scaled, _ = norm_parts(states, attn_gain)
    scaled = scaled.astype(jnp.bfloat16)
    queries = (
        jnp.dot(scaled, w_query, preferred_element_type=jnp.float32)
        .astype(jnp.bfloat16)
        .reshape(requests, step_count, heads_local, head_dim)
    )
    key_new = (
        jnp.dot(scaled, w_key, preferred_element_type=jnp.float32)
        .astype(jnp.bfloat16)
        .reshape(requests, step_count, inner_local)
    )
    value_new = (
        jnp.dot(scaled, w_value, preferred_element_type=jnp.float32)
        .astype(jnp.bfloat16)
        .reshape(requests, step_count, inner_local)
    )
    position = seq_index * span_local + jnp.arange(span_local, dtype=jnp.int32)
    target = lengths[:, None] + jnp.arange(step_count, dtype=jnp.int32)[None, :]
    landing = position[None, None, :] == target[:, :, None]
    landed = jnp.any(landing, axis=1)[:, :, None]
    landing_low = landing.astype(jnp.bfloat16)
    placed_keys = jnp.einsum(
        "rtp,rtc->rpc", landing_low, key_new, preferred_element_type=jnp.float32
    ).astype(jnp.bfloat16)
    placed_values = jnp.einsum(
        "rtp,rtc->rpc", landing_low, value_new, preferred_element_type=jnp.float32
    ).astype(jnp.bfloat16)
    key_rows = jnp.where(landed, placed_keys, cache_keys).reshape(
        requests, span_local, heads_local, head_dim
    )
    value_rows = jnp.where(landed, placed_values, cache_values).reshape(
        requests, span_local, heads_local, head_dim
    )
    scores = jnp.einsum("rthd,rphd->rthp", queries, key_rows, preferred_element_type=jnp.float32)
    bucket_hot = (buckets[..., None] == jnp.arange(bucket_count, dtype=jnp.int32)).astype(
        jnp.float32
    )
    scores = scores + jnp.einsum(
        "rtpb,bh->rthp", bucket_hot, rel_bias, precision=lax.Precision.HIGHEST
    )
    allowed = (position[None, None, :] <= target[:, :, None])[:, :, None, :]
    scores = jnp.where(allowed, scores, -1e30)
    local_top = jnp.max(scores, axis=-1)
    weights = jnp.where(allowed, jnp.exp(scores - local_top[..., None]), 0.0)
    local_mass = jnp.sum(weights, axis=-1)
    partial_value = jnp.einsum(
        "rthp,rphd->rthd", weights, value_rows.astype(jnp.float32), precision=lax.Precision.HIGHEST
    )
    out_rows = w_out.astype(jnp.float32)
    global_top, global_mass, summed = joined(
        (local_top, local_mass, partial_value), "seq", join_three
    )
    heads_out = (summed / global_mass[..., None]).reshape(tokens, inner_local)
    projected = jnp.dot(heads_out, out_rows, precision=lax.Precision.HIGHEST)
    mixed_rows = lax.psum(projected, "head")
    hidden_one = states + mixed_rows
    normed, _ = norm_parts(hidden_one, ffn_gain)
    router_logits = jnp.dot(normed, w_router, precision=lax.Precision.HIGHEST)
    normed_low = normed.astype(jnp.bfloat16)
    expert_total = w_router.shape[1]
    local_experts, model_width, units_local = w_gate.shape
    expert_ids = jnp.arange(expert_total, dtype=jnp.int32)
    pick_marks = (expert_picks[..., None] == expert_ids).astype(jnp.int32)
    per_step = jnp.sum(pick_marks, axis=2)
    earlier = jnp.cumsum(per_step, axis=1) - per_step
    slot_index = jnp.sum(pick_marks * earlier[:, :, None, :], axis=-1)
    pick_total = expert_picks.shape[2]
    token_picks = jnp.transpose(expert_picks, (1, 0, 2)).reshape(tokens, pick_total)
    token_slots = jnp.transpose(slot_index, (1, 0, 2)).reshape(tokens, pick_total)
    token_steps = jnp.arange(tokens, dtype=jnp.int32) % step_count
    picked = jnp.sum(
        jnp.where(token_picks[..., None] == expert_ids, router_logits[:, None, :], 0.0), axis=-1
    )
    gate_first = jax.nn.sigmoid(picked[:, 0] - picked[:, 1])
    gate_second = jax.nn.sigmoid(picked[:, 1] - picked[:, 0])
    slot_rows = step_count * CAP
    row_ids = jnp.arange(local_experts * slot_rows, dtype=jnp.int32)
    row_expert = head_index * local_experts + row_ids // slot_rows
    row_step = row_ids // CAP % step_count
    row_slot = row_ids % CAP
    chooser = jnp.zeros((row_ids.shape[0], tokens), jnp.float32)
    for pick_rank in range(pick_total):
        matched = (
            (row_expert[:, None] == token_picks[None, :, pick_rank])
            & (row_step[:, None] == token_steps[None, :])
            & (row_slot[:, None] == token_slots[None, :, pick_rank])
        )
        chooser = chooser + matched.astype(jnp.float32)
    routed = jnp.dot(
        chooser.astype(jnp.bfloat16), normed_low, preferred_element_type=jnp.float32
    ).astype(jnp.bfloat16)
    routed = routed.reshape(local_experts, slot_rows, model_width)
    gate_part = jnp.einsum("esd,edf->esf", routed, w_gate, preferred_element_type=jnp.float32)
    up_part = jnp.einsum("esd,edf->esf", routed, w_up, preferred_element_type=jnp.float32)
    hidden_units = (jax.nn.gelu(gate_part, approximate=True) * up_part).astype(jnp.bfloat16)
    down_part = jnp.einsum("esf,efd->esd", hidden_units, w_down, preferred_element_type=jnp.float32)
    expert_share = lax.psum_scatter(down_part, "seq", scatter_dimension=2, tiled=True).astype(
        jnp.bfloat16
    )
    share_width = expert_share.shape[2]
    collected = lax.all_gather(expert_share[None], ("seq", "head"), axis=0, tiled=True)
    arranged = collected.reshape(seq_count, head_count, local_experts, slot_rows, share_width)
    arranged = jnp.transpose(arranged, (1, 2, 3, 0, 4)).reshape(
        expert_total * slot_rows, seq_count * share_width
    )
    group_size = tokens // head_count
    first_row = head_index * group_size
    own_picks = lax.dynamic_slice_in_dim(token_picks, first_row, group_size, 0)
    own_slots = lax.dynamic_slice_in_dim(token_slots, first_row, group_size, 0)
    own_steps = lax.dynamic_slice_in_dim(token_steps, first_row, group_size, 0)
    own_first = lax.dynamic_slice_in_dim(gate_first, first_row, group_size, 0)
    own_second = lax.dynamic_slice_in_dim(gate_second, first_row, group_size, 0)
    own_hidden = lax.dynamic_slice_in_dim(hidden_one, first_row, group_size, 0)
    flat_rows = own_picks * slot_rows + own_steps[:, None] * CAP + own_slots
    every_row = jnp.arange(expert_total * slot_rows, dtype=jnp.int32)
    select_first = (flat_rows[:, 0:1] == every_row[None, :]).astype(jnp.bfloat16)
    select_second = (flat_rows[:, 1:2] == every_row[None, :]).astype(jnp.bfloat16)
    expert_mix = own_first[:, None] * jnp.dot(
        select_first, arranged, preferred_element_type=jnp.float32
    )
    expert_mix = expert_mix + own_second[:, None] * jnp.dot(
        select_second, arranged, preferred_element_type=jnp.float32
    )
    final_rows = (own_hidden + expert_mix).astype(jnp.bfloat16)
    scaled_out, norm_root = norm_parts(final_rows.astype(jnp.float32), final_gain)
    logits = jnp.dot(scaled_out.astype(jnp.bfloat16), w_vocab, preferred_element_type=jnp.float32)
    top_logit = lax.pmax(jnp.max(logits, axis=-1), "seq")
    return (final_rows, norm_root, top_logit)


def solution(mesh):
    placed = (
        P(),
        P(),
        P(None, "seq", "head"),
        P(None, "seq", "head"),
        P(None, None, "seq"),
        P(),
        P(None, "head"),
        P(None, "head"),
        P(None, "head"),
        P(None, "head"),
        P("head", None),
        P(),
        P(),
        P("head", None, "seq"),
        P("head", None, "seq"),
        P("head", "seq", None),
        P(),
        P(),
        P(None, "seq"),
    )
    return jax.shard_map(
        shards,
        mesh=mesh,
        in_specs=placed,
        out_specs=(P("head", None), P("head"), P("head")),
        check_vma=False,
    )
```

profile of v0, /device:TPU:32, one launch (start us, length us, event | category | flops | bytes accessed | tf_op | source)
XLA Modules:
  0.0 482.6 jit_solution(6117893066806250847)
XLA Ops:
  7.3 1.2 fusion.13
  9.2 1.3 convolution_convert_fusion.2
  10.7 1.3 convolution_convert_fusion.1
  12.3 4.6 copy.74
  17.0 4.7 copy.77
  22.0 2.0 fusion.4
  24.0 3.1 convert_select_fusion.1
  27.1 1.0 convert_select_fusion
  28.8 3.3 convolution_bitcast_fusion.1
  33.2 25.3 %all-gather.1 = f32[768,4,2]{1,2,0:T(2,128)S(1)} all-gather(f32[24,4,2]{1,2,0:T(2,128)S(1)} %fusion.16), channel_id=3, replica_groups=mesh['seq'=32,'head'=8] {'seq'}, dimensions={0}, use_global_device_ids=true | all-gather | bytes 25344 | tf_op jit(solution)/shard_map/all_gather | solution.py:10
  59.2 25.2 %all-gather = f32[768,4,2]{1,2,0:T(2,128)S(1)} all-gather(f32[24,4,2]{1,2,0:T(2,128)S(1)} %get-tuple-element.240), channel_id=2, replica_groups=mesh['seq'=32,'head'=8] {'seq'}, dimensions={0}, use_global_device_ids=true | all-gather | bytes 25344 | tf_op jit(solution)/shard_map/all_gather | solution.py:10
  84.4 1.2 copy.83
  87.0 76.0 %while.19 = (s32[]{:T(128)}, f32[24,4,2]{0,2,1:T(2,128)S(1)}, f32[24,4,2]{0,2,1:T(2,128)S(1)}, f32[24,4,2,64]{3,2,1,0:T(2,128)S(1)}, f32[32,24,4,2]{1,3,2,0:T(2,...) while((s32[]{:T(128)}, f32[24,4,2]{0,2,1:T(2,128)S(1)}, ...), condition=%wide.region_5.6_spmd, body=%wide.region_4.5_spmd.sunk | while | flops 38021 | bytes 256655 | solution.py:15
  87.9 0.9 constant_dynamic-slice_fusion.6
  90.4 0.9 constant_dynamic-slice_fusion.6
  92.8 0.9 constant_dynamic-slice_fusion.6
  95.3 0.9 constant_dynamic-slice_fusion.6
  97.7 0.9 constant_dynamic-slice_fusion.6
  100.2 0.9 constant_dynamic-slice_fusion.6
  102.6 0.9 constant_dynamic-slice_fusion.6
  105.1 0.9 constant_dynamic-slice_fusion.6
  107.6 0.9 constant_dynamic-slice_fusion.6
  110.0 0.9 constant_dynamic-slice_fusion.6
  112.5 0.9 constant_dynamic-slice_fusion.6
  114.9 0.9 constant_dynamic-slice_fusion.6
  117.4 0.9 constant_dynamic-slice_fusion.6
  119.8 0.9 constant_dynamic-slice_fusion.6
  122.3 0.9 constant_dynamic-slice_fusion.6
  124.7 0.9 constant_dynamic-slice_fusion.6
  127.2 0.9 constant_dynamic-slice_fusion.6
  129.6 0.9 constant_dynamic-slice_fusion.6
  132.1 0.9 constant_dynamic-slice_fusion.6
  134.5 0.9 constant_dynamic-slice_fusion.6
  137.0 0.9 constant_dynamic-slice_fusion.6
  151.7 0.9 constant_dynamic-slice_fusion.6
  156.6 0.9 constant_dynamic-slice_fusion.6
  163.4 1.1 fusion.77
  164.6 72.5 %all-reduce.2.cloned.1.call-done = f32[96,1024]{1,0:T(8,128)} async-done(((f32[96,1024]{1,0:T(8,128)}), f32[96,1024]{1,0:T(8,128)}) %all-reduce.2.cloned.1.call-update) | async-done | bytes 393232 | tf_op jit(solution)/shard_map/psum | solution.py:120
  237.1 1.1 multiply_reduce_fusion
  239.1 1.2 fusion.78
  240.3 2.0 fusion.12
  242.3 1.3 copy.98
  243.6 1.4 reshape.208
  245.2 83.7 %reduce-scatter.4.cloned.1.call-done = f32[32,32]{1,0:T(8,128)} async-done(((f32[1024,32]{1,0:T(8,128)}), f32[32,32]{1,0:T(8,128)}) %reduce-scatter.4.cloned.1.call-update) | async-done | bytes 4112
  329.8 73.4 %all-gather.3 = bf16[512,16,32]{2,1,0:T(8,128)(2,1)S(1)} all-gather(bf16[2,16,32]{2,1,0:T(8,128)(2,1)S(1)} %copy.99), channel_id=5, replica_groups=mesh['seq'=32,'head'=8] {'seq','head'}, dimensions={0}, use_global_device_ids=true | all-gather | bytes 526336 | tf_op jit(solution)/shard_map/all_gather | solution.py:166
  403.2 2.7 copy.112
  405.9 3.5 reshape.189
  410.8 65.3 %pmax.7 = f32[12]{0:T(128)} all-reduce(f32[12]{0:T(128)S(1)} %convolution_reduce_fusion), channel_id=1, replica_groups=mesh['seq'=32,'head'=8] {'seq'}, use_global_device_ids=true, to_apply=%region_15.16 | all-reduce | flops 12 | bytes 96 | tf_op jit(solution)/shard_map/pmax | solution.py:192
  (217 shorter events, 63.7 us)
Async XLA Ops:
  7.2 402.9 %copy-start = (bf16[1024,1004]{0,1:T(8,128)(2,1)S(1)}, bf16[1024,1004]{0,1:T(8,128)(2,1)}, u32[]{:S(2)}) copy-start(bf16[1024,1004]{0,1:T(8,128)(2,1)} %param.39) | copy-start | bytes 6168580
  7.2 4.8 copy-start.2
  7.2 4.8 copy-start.12
  7.2 4.8 copy-start.9
  7.2 78.8 %all-gather.6.cloned.1.call-start = ((), (), s32[]{:S(2)}) async-start(), calls=%async_computation.2 | async-start | bytes 3244032 | tf_op jit(solution)/shard_map/all_gather | solution.py:10
  16.9 5.0 %copy-start.10 = (s32[24,4,512]{2,1,0:T(4,128)S(1)}, s32[24,4,512]{2,1,0:T(4,128)}, u32[]{:S(2)}) copy-start(s32[24,4,512]{2,1,0:T(4,128)} %param.25) | copy-start | bytes 589828
  17.0 5.0 %copy-start.14 = (f32[32,2]{0,1:T(2,128)S(1)}, f32[32,2]{0,1:T(2,128)}, u32[]{:S(2)}) copy-start(f32[32,2]{0,1:T(2,128)} %param.30) | copy-start | bytes 772
  24.0 3.1 copy-start.1
  28.8 3.3 copy-start.6
  32.1 205.0 %all-reduce.2.cloned.1.call-start = ((), (), s32[]{:S(2)}) async-start(), calls=%async_computation.1 | async-start | bytes 786432 | tf_op jit(solution)/shard_map/psum | solution.py:120
  59.1 104.3 %copy-start.4 = (bf16[128,1024]{1,0:T(8,128)(2,1)S(1)}, bf16[128,1024]{1,0:T(8,128)(2,1)}, u32[]{:S(2)}) copy-start(bf16[128,1024]{1,0:T(8,128)(2,1)} %param.31) | copy-start | bytes 786436
  86.9 151.3 %copy-start.11 = (f32[1024,16]{0,1:T(8,128)S(1)}, f32[1024,16]{0,1:T(8,128)}, u32[]{:S(2)}) copy-start(f32[1024,16]{0,1:T(8,128)} %param.33) | copy-start | bytes 196612
  87.0 151.3 %copy-start.13 = (f32[1024]{0:T(1024)S(1)}, f32[1024]{0:T(1024)}, u32[]{:S(2)}) copy-start(f32[1024]{0:T(1024)} %param.32) | copy-start | bytes 12292
  163.0 77.3 %copy-start.3 = (bf16[2,88,1024]{2,1,0:T(8,128)(2,1)S(1)}, bf16[2,88,1024]{2,1,0:T(8,128)(2,1)}, u32[]{:S(2)}) copy-start(bf16[2,88,1024]{2,1,0:T(8,128)(2,1)} %param.36) | copy-start | bytes 1081348
  164.5 164.3 %reduce-scatter.4.cloned.1.call-start = ((), (), s32[]{:S(2)}) async-start(), calls=%async_computation.3 | async-start | bytes 540672
  403.2 6.8 %copy-start.7 = (f32[1024]{0:T(1024)S(1)}, f32[1024]{0:T(1024)}, u32[]{:S(2)}) copy-start(f32[1024]{0:T(1024)} %param.38) | copy-start | bytes 12292
  410.0 66.1 %copy-start.5 = (bf16[12,1024]{1,0:T(8,128)(2,1)}, bf16[12,1024]{1,0:T(8,128)(2,1)S(1)}, u32[]{:S(2)}) copy-start(bf16[12,1024]{1,0:T(8,128)(2,1)S(1)} %get-tuple-element.243) | copy-start | bytes 73732
  410.0 66.1 %copy-start.8 = (f32[12]{0:T(128)}, f32[12]{0:T(128)S(1)}, u32[]{:S(2)}) copy-start(f32[12]{0:T(128)S(1)} %add_sqrt_fusion) | copy-start | bytes 148
Sparse Core Ops, SparseCore 0:
  32.2 53.7 all-gather.5
  164.6 72.4 all-reduce.1
  245.2 83.6 reduce-scatter.3
where the time goes:
time: 485 us; the launch traced here: 483 us
  blocking collectives  189 us (39%)
  waiting for transfers between devices  156 us (32%)
  local copies, waits for them, and re-layouts  58.1 us (12%)
  other arithmetic  44.9 us (9%)
  matrix products  19.3 us (4%)
  between operations  14.1 us (3%)
    unnamed x4, waiting for transfers between devices  83.7 us
    all_gather x1, blocking collectives, shards(): lax.all_gather(expert_share[None], ('seq', 'head'), axis=0, tiled=True)  73.4 us
    psum x1, waiting for transfers between devices, shards(): mixed_rows = lax.psum(projected, 'head')  72.5 us
    pmax x1, blocking collectives, shards(): top_logit = lax.pmax(jnp.max(logits, axis=-1), 'seq')  65.3 us
    all_gather x2, blocking collectives, joined(): gathered = jax.tree.map(lambda a: lax.all_gather(a, axis), part)  50.5 us
    dynamic_slice x34, local copies, waits for them, and re-layouts, take(): lax.dynamic_index_in_dim(a, source, 0, False)  28.9 us
    add x31, other arithmetic, join_three(): mass = earlier_part[1] * lead_scale + later_part[1] * trail_scale  21.9 us
    add x31, other arithmetic, join_three(): earlier_part[2] * lead_scale[..., None]  18.8 us
  transfers between devices with their start and end apart: 3, of which 3 were waited for; matrix products, arithmetic and copies ran while one was open for 1% of the time, Pallas kernels for 0%

commit v1 on v0

--- a/solution.py
+++ b/solution.py
@@ -163,7 +163,12 @@
         jnp.bfloat16
     )
     share_width = expert_share.shape[2]
-    collected = lax.all_gather(expert_share[None], ("seq", "head"), axis=0, tiled=True)
+    collected = jnp.concatenate(
+        lax.all_to_all(
+            jnp.stack([expert_share[None]] * lax.axis_size(("seq", "head"))), ("seq", "head"), 0, 0
+        ),
+        axis=0,
+    )
     arranged = collected.reshape(seq_count, head_count, local_experts, slot_rows, share_width)
     arranged = jnp.transpose(arranged, (1, 2, 3, 0, 4)).reshape(
         expert_total * slot_rows, seq_count * share_width

time: 485 us -> 453 us (0.934)
  blocking collectives: 189 us -> 114 us
  waiting for transfers between devices: 156 us -> 177 us
  starting transfers between devices: 0.12 us -> 11.3 us
  local copies, waits for them, and re-layouts: 58.1 us -> 67.5 us
    all_gather x1 -> x0, blocking collectives: 73.4 us -> none  [shards(): lax.all_gather(expert_share[None], ('seq', 'head'), axis=0, tiled=True)]
    all_to_all x0 -> x1, waiting for transfers between devices: none -> 20 us  [shards(): lax.all_to_all(jnp.stack([expert_share[None]] * lax.axis_size(('seq', 'he...]
    all_to_all x0 -> x1, starting transfers between devices: none -> 11.2 us  [shards(): lax.all_to_all(jnp.stack([expert_share[None]] * lax.axis_size(('seq', 'he...]
    unnamed x36 -> x38, local copies, waits for them, and re-layouts: 13.1 us -> 19.4 us
  transfers between devices with their start and end apart: 3 -> 4, of which waited for: 3 -> 4; matrix products, arithmetic and copies ran while one was open for 1% -> 1% of each run, Pallas kernels for 0% -> 0%
where the time goes in v1:
time: 453 us; the launch traced here: 449 us
  waiting for transfers between devices  177 us (39%)
  blocking collectives  114 us (25%)
  local copies, waits for them, and re-layouts  67.5 us (15%)
  other arithmetic  44.9 us (10%)
  matrix products  19.3 us (4%)
  between operations  14.1 us (3%)
  starting transfers between devices  11.3 us (2%)
    unnamed x4, waiting for transfers between devices  83.8 us
    psum x1, waiting for transfers between devices, shards(): mixed_rows = lax.psum(projected, 'head')  72.9 us
    pmax x1, blocking collectives, shards(): top_logit = lax.pmax(jnp.max(logits, axis=-1), 'seq')  63.6 us
    all_gather x2, blocking collectives, joined(): gathered = jax.tree.map(lambda a: lax.all_gather(a, axis), part)  50.5 us
    dynamic_slice x34, local copies, waits for them, and re-layouts, take(): lax.dynamic_index_in_dim(a, source, 0, False)  28.9 us
    add x31, other arithmetic, join_three(): mass = earlier_part[1] * lead_scale + later_part[1] * trail_scale  21.9 us
    all_to_all x1, waiting for transfers between devices, shards(): lax.all_to_all(jnp.stack([expert_share[None]] * lax.axis_size(('seq', 'he...  20 us
    unnamed x38, local copies, waits for them, and re-layouts  19.4 us
  transfers between devices with their start and end apart: 4, of which 4 were waited for; matrix products, arithmetic and copies ran while one was open for 1% of the time, Pallas kernels for 0%

profile of v1, /device:TPU:32, one launch (start us, length us, event | category | flops | bytes accessed | tf_op | source)
XLA Modules:
  0.0 448.8 jit_solution(6325501579947893515)
XLA Ops:
  7.3 1.2 fusion.13
  9.2 1.3 convolution_convert_fusion.2
  10.7 1.3 convolution_convert_fusion.1
  12.3 4.6 %copy.90 = bf16[24,512,128]{1,2,0:T(8,128)(2,1)} copy(bf16[24,512,128]{2,1,0:T(8,128)(2,1)} %param.23) | data formatting | bytes 6291456 | tf_op args[2]
  17.0 4.7 %copy.93 = bf16[24,512,128]{1,2,0:T(8,128)(2,1)} copy(bf16[24,512,128]{2,1,0:T(8,128)(2,1)} %param.24) | data formatting | bytes 6291456 | tf_op args[3]
  22.0 2.0 fusion.4
  24.0 3.1 convert_select_fusion.1
  27.1 1.0 convert_select_fusion
  28.8 3.3 convolution_bitcast_fusion.1
  33.2 25.3 %all-gather.1 = f32[768,4,2]{1,2,0:T(2,128)S(1)} all-gather(f32[24,4,2]{1,2,0:T(2,128)S(1)} %fusion.16), channel_id=3, replica_groups=mesh['seq'=32,'head'=8] {'seq'}, dimensions={0}, use_global_device_ids=true | all-gather | bytes 25344 | tf_op jit(solution)/shard_map/all_gather | solution.py:10
  59.1 25.2 %all-gather = f32[768,4,2]{1,2,0:T(2,128)S(1)} all-gather(f32[24,4,2]{1,2,0:T(2,128)S(1)} %get-tuple-element.247), channel_id=2, replica_groups=mesh['seq'=32,'head'=8] {'seq'}, dimensions={0}, use_global_device_ids=true | all-gather | bytes 25344 | tf_op jit(solution)/shard_map/all_gather | solution.py:10
  84.4 1.2 copy.99
  87.0 76.0 %while.19 = (s32[]{:T(128)}, f32[24,4,2]{0,2,1:T(2,128)S(1)}, f32[24,4,2]{0,2,1:T(2,128)S(1)}, f32[24,4,2,64]{3,2,1,0:T(2,128)S(1)}, f32[32,24,4,2]{1,3,2,0:T(2,...) while((s32[]{:T(128)}, f32[24,4,2]{0,2,1:T(2,128)S(1)}, ...), condition=%wide.region_5.6_spmd, body=%wide.region_4.5_spmd.sunk | while | flops 38021 | bytes 256655 | solution.py:15
  87.9 0.9 constant_dynamic-slice_fusion.6
  90.4 0.9 constant_dynamic-slice_fusion.6
  92.8 0.9 constant_dynamic-slice_fusion.6
  95.3 0.9 constant_dynamic-slice_fusion.6
  97.7 0.9 constant_dynamic-slice_fusion.6
  100.2 0.9 constant_dynamic-slice_fusion.6
  102.6 0.9 constant_dynamic-slice_fusion.6
  105.1 0.9 constant_dynamic-slice_fusion.6
  107.5 0.9 constant_dynamic-slice_fusion.6
  110.0 0.9 constant_dynamic-slice_fusion.6
  112.4 0.9 constant_dynamic-slice_fusion.6
  114.9 0.9 constant_dynamic-slice_fusion.6
  117.4 0.9 constant_dynamic-slice_fusion.6
  119.8 0.9 constant_dynamic-slice_fusion.6
  122.3 0.9 constant_dynamic-slice_fusion.6
  136.9 0.9 constant_dynamic-slice_fusion.6
  141.9 0.9 constant_dynamic-slice_fusion.6
  146.8 0.9 constant_dynamic-slice_fusion.6
  149.2 0.9 constant_dynamic-slice_fusion.6
  163.4 1.1 fusion.77
  164.6 72.9 %all-reduce.2.cloned.1.call-done = f32[96,1024]{1,0:T(8,128)} async-done(((f32[96,1024]{1,0:T(8,128)}), f32[96,1024]{1,0:T(8,128)}) %all-reduce.2.cloned.1.call-update) | async-done | bytes 393232 | tf_op jit(solution)/shard_map/psum | solution.py:120
  237.5 1.1 multiply_reduce_fusion
  238.9 1.2 fusion.78
  240.1 2.0 fusion.12
  242.1 1.3 copy.114
  243.5 1.4 reshape.204
  245.0 83.7 %reduce-scatter.4.cloned.1.call-done = f32[32,32]{1,0:T(8,128)} async-done(((f32[1024,32]{1,0:T(8,128)}), f32[32,32]{1,0:T(8,128)}) %reduce-scatter.4.cloned.1.call-update) | async-done | bytes 4112
  329.6 1.6 stack.3
  331.2 4.3 reshape.206
  335.5 11.2 %all-to-all-start = ((bf16[256,2,512]{2,1,0:T(2,128)(2,1)}), bf16[256,2,512]{2,1,0:T(2,128)(2,1)S(1)}, u32[]{:S(2)}, u32[]{:S(2)}) async-start(bf16[256,2,512]{2,1,0:T(2,128)(2,1)} %reshape.206), calls=%async_computation | async-start | bytes 1048576 | tf_op jit(solution)/shard_map/all_to_all | solution.py:167
  347.4 20.0 %all-to-all-done = bf16[256,2,512]{2,1,0:T(2,128)(2,1)S(1)} async-done(((bf16[256,2,512]{2,1,0:T(2,128)(2,1)}), bf16[256,2,512]{2,1,0:T(2,128)(2,1)S(1)}, u32[]{:S(2)}, u32[]{:S(2)}) %all-to-all-start) | async-done | bytes 524320 | tf_op jit(solution)/shard_map/all_to_all | solution.py:167
  367.4 2.1 reshape.207
  369.5 4.2 copy.108
  373.7 3.5 reshape.187
  378.7 63.6 %pmax.7 = f32[12]{0:T(128)} all-reduce(f32[12]{0:T(128)S(1)} %convolution_reduce_fusion), channel_id=1, replica_groups=mesh['seq'=32,'head'=8] {'seq'}, use_global_device_ids=true, to_apply=%region_15.16 | all-reduce | flops 12 | bytes 96 | tf_op jit(solution)/shard_map/pmax | solution.py:197
  (220 shorter events, 67.4 us)
Async XLA Ops:
  7.2 370.7 %copy-start = (bf16[1024,1004]{0,1:T(8,128)(2,1)S(1)}, bf16[1024,1004]{0,1:T(8,128)(2,1)}, u32[]{:S(2)}) copy-start(bf16[1024,1004]{0,1:T(8,128)(2,1)} %param.39) | copy-start | bytes 6168580
  7.2 4.8 %copy-start.2 = (bf16[96,1024]{1,0:T(8,128)(2,1)S(1)}, bf16[96,1024]{1,0:T(8,128)(2,1)}, u32[]{:S(2)}) copy-start(bf16[96,1024]{1,0:T(8,128)(2,1)} %param.21) | copy-start | bytes 589828
  7.2 4.8 %copy-start.12 = (f32[1024]{0:T(1024)S(1)}, f32[1024]{0:T(1024)}, u32[]{:S(2)}) copy-start(f32[1024]{0:T(1024)} %param.26) | copy-start | bytes 12292
  7.2 4.8 %copy-start.9 = (bf16[1024,128]{1,0:T(8,128)(2,1)S(1)}, bf16[1024,128]{1,0:T(8,128)(2,1)}, u32[]{:S(2)}) copy-start(bf16[1024,128]{1,0:T(8,128)(2,1)} %param.28) | copy-start | bytes 786436
  7.2 78.8 %all-gather.5.cloned.1.call-start = ((), (), s32[]{:S(2)}) async-start(), calls=%async_computation.3 | async-start | bytes 3244032 | tf_op jit(solution)/shard_map/all_gather | solution.py:10
  16.9 5.0 %copy-start.10 = (s32[24,4,512]{2,1,0:T(4,128)S(1)}, s32[24,4,512]{2,1,0:T(4,128)}, u32[]{:S(2)}) copy-start(s32[24,4,512]{2,1,0:T(4,128)} %param.25) | copy-start | bytes 589828
  17.0 5.0 %copy-start.14 = (f32[32,2]{0,1:T(2,128)S(1)}, f32[32,2]{0,1:T(2,128)}, u32[]{:S(2)}) copy-start(f32[32,2]{0,1:T(2,128)} %param.30) | copy-start | bytes 772
  24.0 3.1 copy-start.1
  28.8 3.3 copy-start.6
  32.1 205.4 %all-reduce.2.cloned.1.call-start = ((), (), s32[]{:S(2)}) async-start(), calls=%async_computation.2 | async-start | bytes 786432 | tf_op jit(solution)/shard_map/psum | solution.py:120
  59.1 104.3 %copy-start.4 = (bf16[128,1024]{1,0:T(8,128)(2,1)S(1)}, bf16[128,1024]{1,0:T(8,128)(2,1)}, u32[]{:S(2)}) copy-start(bf16[128,1024]{1,0:T(8,128)(2,1)} %param.31) | copy-start | bytes 786436
  86.9 151.7 %copy-start.13 = (f32[1024]{0:T(1024)S(1)}, f32[1024]{0:T(1024)}, u32[]{:S(2)}) copy-start(f32[1024]{0:T(1024)} %param.32) | copy-start | bytes 12292
  163.0 77.1 %copy-start.3 = (bf16[2,88,1024]{2,1,0:T(8,128)(2,1)S(1)}, bf16[2,88,1024]{2,1,0:T(8,128)(2,1)}, u32[]{:S(2)}) copy-start(bf16[2,88,1024]{2,1,0:T(8,128)(2,1)} %param.36) | copy-start | bytes 1081348
  164.5 164.2 %reduce-scatter.4.cloned.1.call-start = ((), (), s32[]{:S(2)}) async-start(), calls=%async_computation.4 | async-start | bytes 540672
  244.9 101.9 %copy-start.11 = (f32[1024,16]{0,1:T(8,128)S(1)}, f32[1024,16]{0,1:T(8,128)}, u32[]{:S(2)}) copy-start(f32[1024,16]{0,1:T(8,128)} %param.33) | copy-start | bytes 196612
  335.5 31.9 %all-to-all-start = ((bf16[256,2,512]{2,1,0:T(2,128)(2,1)}), bf16[256,2,512]{2,1,0:T(2,128)(2,1)S(1)}, u32[]{:S(2)}, u32[]{:S(2)}) async-start(bf16[256,2,512]{2,1,0:T(2,128)(2,1)} %reshape.206), calls=%async_computation | async-start | bytes 1048576 | tf_op jit(solution)/shard_map/all_to_all | solution.py:167
  369.5 8.4 %copy-start.7 = (f32[1024]{0:T(1024)S(1)}, f32[1024]{0:T(1024)}, u32[]{:S(2)}) copy-start(f32[1024]{0:T(1024)} %param.38) | copy-start | bytes 12292
  377.8 64.4 %copy-start.5 = (bf16[12,1024]{1,0:T(8,128)(2,1)}, bf16[12,1024]{1,0:T(8,128)(2,1)S(1)}, u32[]{:S(2)}) copy-start(bf16[12,1024]{1,0:T(8,128)(2,1)S(1)} %get-tuple-element.250) | copy-start | bytes 73732
  377.8 64.4 %copy-start.8 = (f32[12]{0:T(128)}, f32[12]{0:T(128)S(1)}, u32[]{:S(2)}) copy-start(f32[12]{0:T(128)S(1)} %add_sqrt_fusion) | copy-start | bytes 148
Sparse Core Ops, SparseCore 0:
  32.2 53.7 all-gather.4
  164.6 72.8 all-reduce.1
  245.0 83.6 reduce-scatter.3
